TPU v7x, 32 devices: a whole 2x2x4 slice. The times are simulated.
32 devices in a mesh: rep: 2 (over core), shard: 16 (over z, y, x).
Axes of the slice: x: 2, y: 2, z: 4, core: 2. Of those that a mesh axis runs over, the one named last changes fastest.
Arguments:
- tokens: bfloat16 [12288, 1536], P(('rep', 'shard')), may hold values from -6 to 6
- prompt_ids: int32 [32, 4], P(('rep', 'shard')), may hold values from 0 to 1
- seq_offsets: int32 [32, 4], P(('rep', 'shard')), may hold values from 32 to 64, as said below
- attn_gain: bfloat16 [1536], P('shard'), may hold values from 0.5 to 1.5
- w_query: bfloat16 [1536, 1536], P('shard'), may hold values from -0.15625 to 0.15625
- w_key: bfloat16 [1536, 1536], P('shard'), may hold values from -0.15625 to 0.15625
- w_value: bfloat16 [1536, 1536], P('shard'), may hold values from -0.15625 to 0.15625
- w_outgate: bfloat16 [1536, 1536], P('shard'), may hold values from -0.15625 to 0.15625
- w_forget: bfloat16 [1536, 24], P('shard'), may hold values from -0.15625 to 0.15625
- forget_bias: bfloat16 [24], replicated, may hold values from 1 to 8
- w_output: bfloat16 [1536, 1536], P('shard'), may hold values from -0.625 to 0.625
- ffn_gain: bfloat16 [1536], P('shard'), may hold values from 0.5 to 1.5
- w_gate: bfloat16 [1536, 4096], P('shard'), may hold values from -0.15625 to 0.15625
- w_up: bfloat16 [1536, 4096], P('shard'), may hold values from -0.15625 to 0.15625
- w_down: bfloat16 [4096, 1536], P('shard'), may hold values from -0.09375 to 0.09375
- cotangent: bfloat16 [12288, 1536], P(('rep', 'shard')), may hold values from -6 to 6
Outputs:
- layer_out: bfloat16 [12288, 1536], P(('rep', 'shard'))
- tokens_grad: float32 [12288, 1536], P(('rep', 'shard'))
- attn_gain_grad: float32 [1536], P('shard')
- query_grad: float32 [1536, 1536], P('shard')
- key_grad: float32 [1536, 1536], P('shard')
- value_grad: float32 [1536, 1536], P('shard')
- outgate_grad: float32 [1536, 1536], P('shard')
- forget_grad: float32 [1536, 24], P('shard')
- forget_bias_grad: float32 [24], replicated
- output_grad: float32 [1536, 1536], P('shard')
- ffn_gain_grad: float32 [1536], P('shard')
- gate_grad: float32 [1536, 4096], P('shard')
- up_grad: float32 [1536, 4096], P('shard')
- down_grad: float32 [4096, 1536], P('shard')
Inputs may be any that keep to these rules, and one draw needn't show every extreme that they name: `prompt_ids`: each continuation follows one of the 2 prompts of its own block. `seq_offsets`: in every block at least one continuation follows its whole prompt.
All inputs are finite; a program needn't handle non-finite values.
Results may differ from a plain program's by a relative error of at most 0.023.
Values may be sent and summed in bfloat16 or wider, within the bound.
No kernel may reach another device: no remote copies, remote signals or barrier semaphores. Data moves between devices by JAX's collectives and lax.ppermute only.
A program may use at most 320 MiB of HBM per device.

v0:
```python
import jax
import jax.numpy as jnp
from jax import lax
from jax.sharding import PartitionSpec as P

PLEN = 64
CLEN = 64
NP = 2
NC = 4
EPS = 1e-06
NEGATIVE = -1e30


def chain_mask(prompt_ids, offsets):
    positions = jnp.arange(NP * PLEN + NC * CLEN, dtype=jnp.int32)
    in_prompt = positions < NP * PLEN
    after_prompts = positions - NP * PLEN
    sequence = jnp.where(in_prompt, positions // PLEN, NP + after_prompts // CLEN)
    within = jnp.where(in_prompt, positions % PLEN, after_prompts % CLEN)
    cont_index = sequence - NP
    selector = (cont_index[:, None] == jnp.arange(NC, dtype=jnp.int32)[None, :]).astype(jnp.int32)
    owner_id = jnp.where(in_prompt, -1, jnp.sum(selector * prompt_ids[None, :], axis=1))
    reach_end = jnp.sum(selector * offsets[None, :], axis=1)
    same_seq = (sequence[:, None] == sequence[None, :]) & (within[None, :] <= within[:, None])
    from_prompt = (owner_id[:, None] == sequence[None, :]) & (within[None, :] < reach_end[:, None])
    return same_seq | from_prompt


def normalize(values):
    inverse = lax.rsqrt(jnp.mean(values * values, axis=1, keepdims=True) + EPS)
    return (values * inverse, inverse)


def norm_back(grad_scaled, scaled, inverse):
    return inverse * (grad_scaled - scaled * jnp.mean(grad_scaled * scaled, axis=1, keepdims=True))


def matmul(left_side, right_side):
    return jnp.dot(left_side, right_side, preferred_element_type=jnp.float32)


def matmul_tn(left_side, right_side):
    return lax.dot_general(
        left_side, right_side, (((0,), (0,)), ((), ())), preferred_element_type=jnp.float32
    )


def matmul_nt(left_side, right_side):
    return lax.dot_general(
        left_side, right_side, (((1,), (1,)), ((), ())), preferred_element_type=jnp.float32
    )


def decayed_scores(query_low, key_low, decay_sum, chain_ok, score_scale):
    logits = jnp.einsum("qhd,khd->hqk", query_low, key_low, preferred_element_type=jnp.float32)
    decay_t = decay_sum.T
    logits = logits * score_scale + decay_t[:, :, None] - decay_t[:, None, :]
    return jnp.where(chain_ok[None, :, :], logits, NEGATIVE)


def local(
    tokens,
    prompt_ids,
    seq_offsets,
    attn_gain,
    w_query,
    w_key,
    w_value,
    w_outgate,
    w_forget,
    forget_bias,
    w_output,
    ffn_gain,
    w_gate,
    w_up,
    w_down,
    cotangent,
):
    row_count = tokens.shape[0]
    model_width = tokens.shape[1]
    head_count = w_forget.shape[1]
    head_dim = model_width // head_count
    score_scale = head_dim ** (-0.5)
    chain_ok = chain_mask(prompt_ids[0], seq_offsets[0])
    chain_float = chain_ok.astype(jnp.float32)
    inputs = tokens.astype(jnp.float32)
    scaled1, inverse1 = normalize(inputs)
    gain_part = lax.all_gather(attn_gain, "shard", axis=0, tiled=True)
    query_part = lax.all_gather(w_query, "shard", axis=0, tiled=True)
    key_part = lax.all_gather(w_key, "shard", axis=0, tiled=True)
    value_part = lax.all_gather(w_value, "shard", axis=0, tiled=True)
    outgate_part = lax.all_gather(w_outgate, "shard", axis=0, tiled=True)
    forget_part = lax.all_gather(w_forget, "shard", axis=0, tiled=True)
    normed_part = (scaled1 * gain_part.astype(jnp.float32)).astype(jnp.bfloat16)
    gain_one = gain_part
    normed1 = normed_part
    query_proj = matmul(normed_part, query_part)
    key_proj = matmul(normed_part, key_part)
    value_proj = matmul(normed_part, value_part)
    outgate_pre = matmul(normed_part, outgate_part)
    forget_pre = matmul(normed_part, forget_part)
    query_low = query_proj.astype(jnp.bfloat16).reshape(row_count, head_count, head_dim)
    key_low = key_proj.astype(jnp.bfloat16).reshape(row_count, head_count, head_dim)
    value_low = value_proj.astype(jnp.bfloat16).reshape(row_count, head_count, head_dim)
    forget_in = forget_pre + forget_bias.astype(jnp.float32)[None, :]
    decay_sum = jnp.dot(chain_float, jax.nn.log_sigmoid(forget_in), precision=lax.Precision.HIGHEST)
    logits = decayed_scores(query_low, key_low, decay_sum, chain_ok, score_scale)
    top_score = jnp.max(logits, axis=2, keepdims=True)
    exp_scores = jnp.exp(logits - top_score)
    denominator = jnp.sum(exp_scores, axis=2, keepdims=True)
    log_total = top_score + jnp.log(denominator)
    probs_low = (exp_scores / denominator).astype(jnp.bfloat16)
    attended = jnp.einsum(
        "hqk,khd->qhd", probs_low, value_low, preferred_element_type=jnp.float32
    ).reshape(row_count, model_width)
    gate_open = jax.nn.sigmoid(outgate_pre)
    gated_low = (attended * gate_open).astype(jnp.bfloat16)
    branch_attn = matmul(gated_low, lax.all_gather(w_output, "shard", axis=0, tiled=True))
    residual = inputs + branch_attn
    scaled2, inverse2 = normalize(residual)
    gain_part = lax.all_gather(ffn_gain, "shard", axis=0, tiled=True)
    gate_part = lax.all_gather(w_gate, "shard", axis=0, tiled=True)
    up_part = lax.all_gather(w_up, "shard", axis=0, tiled=True)
    normed_part = (scaled2 * gain_part.astype(jnp.float32)).astype(jnp.bfloat16)
    gate_pre = matmul(normed_part, gate_part)
    up_pre = matmul(normed_part, up_part)
    sig_gate = jax.nn.sigmoid(gate_pre)
    silu_gate = gate_pre * sig_gate
    act_low = (silu_gate * up_pre).astype(jnp.bfloat16)
    branch_ffn = matmul(act_low, lax.all_gather(w_down, "shard", axis=0, tiled=True))
    layer_out = (residual + branch_ffn).astype(jnp.bfloat16)
    grad_out = cotangent.astype(jnp.float32)
    grad_act = matmul_nt(cotangent, lax.all_gather(w_down, "shard", axis=0, tiled=True))
    grad_gate = (grad_act * up_pre * sig_gate * (1.0 + gate_pre * (1.0 - sig_gate))).astype(
        jnp.bfloat16
    )
    grad_up = (grad_act * silu_gate).astype(jnp.bfloat16)
    gate_part = lax.all_gather(w_gate, "shard", axis=0, tiled=True)
    up_part = lax.all_gather(w_up, "shard", axis=0, tiled=True)
    contribution = matmul_nt(grad_gate, gate_part) + matmul_nt(grad_up, up_part)
    grad_normed2 = contribution
    grad_down = matmul_tn(act_low, cotangent)
    grad_gate_w = matmul_tn(normed_part, grad_gate)
    grad_up_w = matmul_tn(normed_part, grad_up)
    grad_gain2 = jnp.sum(grad_normed2 * scaled2, axis=0)
    ffn_parts = (
        lax.psum_scatter(
            grad_gain2.astype(jnp.bfloat16), "shard", scatter_dimension=0, tiled=True
        ).astype(jnp.float32),
        lax.psum_scatter(
            grad_gate_w.astype(jnp.bfloat16), "shard", scatter_dimension=0, tiled=True
        ).astype(jnp.float32),
        lax.psum_scatter(
            grad_up_w.astype(jnp.bfloat16), "shard", scatter_dimension=0, tiled=True
        ).astype(jnp.float32),
        lax.psum_scatter(
            grad_down.astype(jnp.bfloat16), "shard", scatter_dimension=0, tiled=True
        ).astype(jnp.float32),
    )
    grad_resid = grad_out + norm_back(
        grad_normed2 * gain_part.astype(jnp.float32), scaled2, inverse2
    )
    grad_attn = grad_resid.astype(jnp.bfloat16)
    grad_gated = matmul_nt(grad_attn, lax.all_gather(w_output, "shard", axis=0, tiled=True))
    grad_output_w = matmul_tn(gated_low, grad_attn)
    grad_attended = (
        (grad_gated * gate_open).astype(jnp.bfloat16).reshape(row_count, head_count, head_dim)
    )
    grad_outgate = (grad_gated * attended * gate_open * (1.0 - gate_open)).astype(jnp.bfloat16)
    logits = decayed_scores(query_low, key_low, decay_sum, chain_ok, score_scale)
    prob_full = jnp.exp(logits - log_total)
    prob_again = prob_full.astype(jnp.bfloat16)
    grad_probs = jnp.einsum(
        "qhd,khd->hqk", grad_attended, value_low, preferred_element_type=jnp.float32
    )
    grad_value = jnp.einsum(
        "hqk,qhd->khd", prob_again, grad_attended, preferred_element_type=jnp.float32
    )
    grad_logits = prob_full * (grad_probs - jnp.sum(prob_full * grad_probs, axis=2, keepdims=True))
    grad_qk = (grad_logits * score_scale).astype(jnp.bfloat16)
    grad_query = jnp.einsum("hqk,khd->qhd", grad_qk, key_low, preferred_element_type=jnp.float32)
    grad_key = jnp.einsum("hqk,qhd->khd", grad_qk, query_low, preferred_element_type=jnp.float32)
    grad_decay = (jnp.sum(grad_logits, axis=2) - jnp.sum(grad_logits, axis=1)).T
    grad_log_forget = lax.dot_general(
        chain_float, grad_decay, (((0,), (0,)), ((), ())), precision=lax.Precision.HIGHEST
    )
    grad_forget_in = grad_log_forget * jax.nn.sigmoid(-forget_in)
    grad_bias = lax.psum(jnp.sum(grad_forget_in, axis=0), ("rep", "shard"))
    grad_query_low = grad_query.reshape(row_count, model_width).astype(jnp.bfloat16)
    grad_key_low = grad_key.reshape(row_count, model_width).astype(jnp.bfloat16)
    grad_value_low = grad_value.reshape(row_count, model_width).astype(jnp.bfloat16)
    grad_forget_low = grad_forget_in.astype(jnp.bfloat16)
    query_part = lax.all_gather(w_query, "shard", axis=0, tiled=True)
    key_part = lax.all_gather(w_key, "shard", axis=0, tiled=True)
    value_part = lax.all_gather(w_value, "shard", axis=0, tiled=True)
    outgate_part = lax.all_gather(w_outgate, "shard", axis=0, tiled=True)
    forget_part = lax.all_gather(w_forget, "shard", axis=0, tiled=True)
    contribution = (
        matmul_nt(grad_query_low, query_part)
        + matmul_nt(grad_key_low, key_part)
        + matmul_nt(grad_value_low, value_part)
        + matmul_nt(grad_outgate, outgate_part)
        + matmul_nt(grad_forget_low, forget_part)
    )
    grad_query_w = matmul_tn(normed1, grad_query_low)
    grad_key_w = matmul_tn(normed1, grad_key_low)
    grad_value_w = matmul_tn(normed1, grad_value_low)
    grad_outgate_w = matmul_tn(normed1, grad_outgate)
    grad_forget_w = matmul_tn(normed1, grad_forget_low)
    grad_gain1 = jnp.sum(contribution * scaled1, axis=0)
    grad_inputs = grad_resid + norm_back(
        contribution * gain_one.astype(jnp.float32), scaled1, inverse1
    )
    attn_parts = (
        lax.psum_scatter(
            grad_gain1.astype(jnp.bfloat16), "shard", scatter_dimension=0, tiled=True
        ).astype(jnp.float32),
        lax.psum_scatter(
            grad_query_w.astype(jnp.bfloat16), "shard", scatter_dimension=0, tiled=True
        ).astype(jnp.float32),
        lax.psum_scatter(
            grad_key_w.astype(jnp.bfloat16), "shard", scatter_dimension=0, tiled=True
        ).astype(jnp.float32),
        lax.psum_scatter(
            grad_value_w.astype(jnp.bfloat16), "shard", scatter_dimension=0, tiled=True
        ).astype(jnp.float32),
        lax.psum_scatter(
            grad_outgate_w.astype(jnp.bfloat16), "shard", scatter_dimension=0, tiled=True
        ).astype(jnp.float32),
        lax.psum_scatter(
            grad_forget_w.astype(jnp.bfloat16), "shard", scatter_dimension=0, tiled=True
        ).astype(jnp.float32),
        lax.psum_scatter(
            grad_output_w.astype(jnp.bfloat16), "shard", scatter_dimension=0, tiled=True
        ).astype(jnp.float32),
    )
    summed = (
        lax.psum(attn_parts[0].astype(jnp.bfloat16), "rep").astype(jnp.float32),
        lax.psum(attn_parts[1].astype(jnp.bfloat16), "rep").astype(jnp.float32),
        lax.psum(attn_parts[2].astype(jnp.bfloat16), "rep").astype(jnp.float32),
        lax.psum(attn_parts[3].astype(jnp.bfloat16), "rep").astype(jnp.float32),
        lax.psum(attn_parts[4].astype(jnp.bfloat16), "rep").astype(jnp.float32),
        lax.psum(attn_parts[5].astype(jnp.bfloat16), "rep").astype(jnp.float32),
        lax.psum(attn_parts[6].astype(jnp.bfloat16), "rep").astype(jnp.float32),
        lax.psum(ffn_parts[0].astype(jnp.bfloat16), "rep").astype(jnp.float32),
        lax.psum(ffn_parts[1].astype(jnp.bfloat16), "rep").astype(jnp.float32),
        lax.psum(ffn_parts[2].astype(jnp.bfloat16), "rep").astype(jnp.float32),
        lax.psum(ffn_parts[3].astype(jnp.bfloat16), "rep").astype(jnp.float32),
    )
    return (
        layer_out,
        grad_inputs,
        summed[0],
        summed[1],
        summed[2],
        summed[3],
        summed[4],
        summed[5],
        grad_bias,
        summed[6],
        summed[7],
        summed[8],
        summed[9],
        summed[10],
    )


def solution(mesh):
    in_specs = (
        P(("rep", "shard"), None),
        P(("rep", "shard"), None),
        P(("rep", "shard"), None),
        P("shard"),
        P("shard", None),
        P("shard", None),
        P("shard", None),
        P("shard", None),
        P("shard", None),
        P(),
        P("shard", None),
        P("shard"),
        P("shard", None),
        P("shard", None),
        P("shard", None),
        P(("rep", "shard"), None),
    )
    out_specs = (
        P(("rep", "shard"), None),
        P(("rep", "shard"), None),
        P("shard"),
        P("shard", None),
        P("shard", None),
        P("shard", None),
        P("shard", None),
        P("shard", None),
        P(),
        P("shard", None),
        P("shard"),
        P("shard", None),
        P("shard", None),
        P("shard", None),
    )
    return jax.shard_map(local, mesh=mesh, in_specs=in_specs, out_specs=out_specs, check_vma=False)
```

profile of v0, /device:TPU:0, one launch (start us, length us, event | category | flops | bytes accessed | tf_op | source)
XLA Modules:
  0.0 2422.7 jit_solution(16868182657455146212)
XLA Ops:
  14.6 45.2 %all-reduce.5 = (bf16[1536]{0:T(1024)(128)(2,1)S(1)}, bf16[1536]{0:T(1024)(128)(2,1)S(1)}) all-reduce(bf16[1536]{0:T(1024)(128)(2,1)S(1)} %dynamic-update-slice, bf16[1536]{0:T(1024)(128)(2,1)S(1)} %dynamic-update-slice.1), channel_id=1, replica_groups=mesh['rep'=2,'shard'=16] {'shard'}, use_global_device_ids=true, to_apply=%add | all-reduce | flops 3072 | bytes 12288
  59.8 37.5 %all-gather = bf16[16,96,24]{1,2,0:T(8,128)(2,1)S(1)} all-gather(bf16[1,96,24]{1,2,0:T(8,128)(2,1)S(1)} %bitcast.93), channel_id=1, replica_groups=mesh['rep'=2,'shard'=16] {'shard'}, dimensions={0}, use_global_device_ids=true | all-gather | bytes 78336 | tf_op jit(solution)/shard_map/all_gather | solution.py:93
  105.3 71.1 %all-gather.14.cloned.1.call-done = bf16[1536,1536]{1,0:T(8,128)(2,1)} async-done(((bf16[96,1536]{1,0:T(8,128)(2,1)}), bf16[1536,1536]{1,0:T(8,128)(2,1)}) %all-gather.14.cloned.1.call-update) | async-done | bytes 4718608 | tf_op jit(solution)/shard_map/all_gather | solution.py:90
  183.5 74.1 %all-gather.10.cloned.1.call-done = bf16[1536,1536]{1,0:T(8,128)(2,1)} async-done(((bf16[96,1536]{1,0:T(8,128)(2,1)}), bf16[1536,1536]{1,0:T(8,128)(2,1)}) %all-gather.10.cloned.1.call-update) | async-done | bytes 4718608 | tf_op jit(solution)/shard_map/all_gather | solution.py:91
  280.6 9.0 fusion.10
  292.0 46.6 %all-gather.16.cloned.1.call-done = bf16[1536,1536]{1,0:T(8,128)(2,1)} async-done(((bf16[96,1536]{1,0:T(8,128)(2,1)}), bf16[1536,1536]{1,0:T(8,128)(2,1)}) %all-gather.16.cloned.1.call-update) | async-done | bytes 4718608 | tf_op jit(solution)/shard_map/all_gather | solution.py:92
  345.1 74.6 %all-gather.18.cloned.1.call-done = bf16[1536,1536]{1,0:T(8,128)(2,1)} async-done(((bf16[96,1536]{1,0:T(8,128)(2,1)}), bf16[1536,1536]{1,0:T(8,128)(2,1)}) %all-gather.18.cloned.1.call-update) | async-done | bytes 4718608 | tf_op jit(solution)/shard_map/all_gather | solution.py:118
  426.4 146.0 %all-gather.22.cloned.1.call-done = bf16[1536,4096]{1,0:T(8,128)(2,1)} async-done(((bf16[96,4096]{1,0:T(8,128)(2,1)}), bf16[1536,4096]{1,0:T(8,128)(2,1)}) %all-gather.22.cloned.1.call-update) | async-done | bytes 12582928 | tf_op jit(solution)/shard_map/all_gather | solution.py:123
  572.4 9.9 fusion.88
  582.3 142.5 %all-gather.20.cloned.1.call-done = bf16[1536,4096]{1,0:T(8,128)(2,1)} async-done(((bf16[96,4096]{1,0:T(8,128)(2,1)}), bf16[1536,4096]{1,0:T(8,128)(2,1)}) %all-gather.20.cloned.1.call-update) | async-done | bytes 12582928 | tf_op jit(solution)/shard_map/all_gather | solution.py:122
  724.8 9.9 fusion.87
  734.7 142.5 %all-gather.24.cloned.1.call-done = bf16[4096,1536]{1,0:T(8,128)(2,1)} async-done(((bf16[256,1536]{1,0:T(8,128)(2,1)}), bf16[4096,1536]{1,0:T(8,128)(2,1)}) %all-gather.24.cloned.1.call-update) | async-done | bytes 12582928 | tf_op jit(solution)/shard_map/all_gather | solution.py:130
  877.2 15.0 multiply_convert_fusion.1
  892.2 9.7 fusion.89
  902.0 9.3 multiply_reduce_fusion.1
  948.4 22.3 fusion.83
  970.7 8.2 fusion.30
  997.1 11.3 convolution_convert_fusion
  1008.5 11.3 convolution_convert_fusion.1
  1020.0 11.4 convolution_convert_fusion.2
  1048.1 38.9 %psum.90 = f32[24]{0:T(128)} all-reduce(f32[24]{0:T(128)S(1)} %get-tuple-element.53), channel_id=1, replica_groups=mesh['rep'=2,'shard'=16] {'rep','shard'}, use_global_device_ids=true, to_apply=%region_25.26 | all-reduce | flops 24 | bytes 192 | tf_op jit(solution)/shard_map/psum | solution.py:188
  1086.9 110.5 %reduce-scatter.18.cloned.1.call-done = bf16[96,1536]{1,0:T(8,128)(2,1)} async-done(((bf16[1536,1536]{1,0:T(8,128)(2,1)}), bf16[96,1536]{1,0:T(8,128)(2,1)}) %reduce-scatter.18.cloned.1.call-update) | async-done | bytes 294928 | tf_op jit(solution)/shard_map/reduce_scatter | solution.py:227
  1197.4 143.3 %reduce-scatter.16.cloned.1.call-done = bf16[96,1536]{1,0:T(8,128)(2,1)} async-done(((bf16[1536,1536]{1,0:T(8,128)(2,1)}), bf16[96,1536]{1,0:T(8,128)(2,1)}) %reduce-scatter.16.cloned.1.call-update) | async-done | bytes 294928 | tf_op jit(solution)/shard_map/reduce_scatter | solution.py:224
  1340.7 142.9 %reduce-scatter.14.cloned.1.call-done = bf16[96,1536]{1,0:T(8,128)(2,1)} async-done(((bf16[1536,1536]{1,0:T(8,128)(2,1)}), bf16[96,1536]{1,0:T(8,128)(2,1)}) %reduce-scatter.14.cloned.1.call-update) | async-done | bytes 294928 | tf_op jit(solution)/shard_map/reduce_scatter | solution.py:221
  1483.7 143.1 %reduce-scatter.12.cloned.1.call-done = bf16[96,1536]{1,0:T(8,128)(2,1)} async-done(((bf16[1536,1536]{1,0:T(8,128)(2,1)}), bf16[96,1536]{1,0:T(8,128)(2,1)}) %reduce-scatter.12.cloned.1.call-update) | async-done | bytes 294928 | tf_op jit(solution)/shard_map/reduce_scatter | solution.py:218
  1626.7 207.2 %reduce-scatter.26.cloned.1.call-done = bf16[256,1536]{1,0:T(8,128)(2,1)} async-done(((bf16[4096,1536]{1,0:T(8,128)(2,1)}), bf16[256,1536]{1,0:T(8,128)(2,1)}) %reduce-scatter.26.cloned.1.call-update) | async-done | bytes 786448 | tf_op jit(solution)/shard_map/reduce_scatter | solution.py:156
  1834.0 207.7 %reduce-scatter.24.cloned.1.call-done = bf16[96,4096]{1,0:T(8,128)(2,1)} async-done(((bf16[1536,4096]{1,0:T(8,128)(2,1)}), bf16[96,4096]{1,0:T(8,128)(2,1)}) %reduce-scatter.24.cloned.1.call-update) | async-done | bytes 786448 | tf_op jit(solution)/shard_map/reduce_scatter | solution.py:153
  2041.7 207.7 %reduce-scatter.22.cloned.1.call-done = bf16[96,4096]{1,0:T(8,128)(2,1)} async-done(((bf16[1536,4096]{1,0:T(8,128)(2,1)}), bf16[96,4096]{1,0:T(8,128)(2,1)}) %reduce-scatter.22.cloned.1.call-update) | async-done | bytes 786448 | tf_op jit(solution)/shard_map/reduce_scatter | solution.py:150
  2262.4 41.8 %all-reduce.4 = (bf16[1536]{0:T(1024)(128)(2,1)}, bf16[1536]{0:T(1024)(128)(2,1)}) all-reduce(bf16[1536]{0:T(1024)(128)(2,1)S(1)} %get-tuple-element.18, bf16[1536]{0:T(1024)(128)(2,1)} %get-tuple-element.16), channel_id=2, replica_groups=mesh['rep'=2,'shard'=16] {'shard'}, use_global_device_ids=true, to_apply=%region_12.13.clone | all-reduce | flops 3072 | bytes 12288
  2310.8 9.3 fusion.19
  2320.1 56.9 %reduce-scatter.28.cloned.1.call-done = bf16[96,24]{1,0:T(8,128)(2,1)} async-done(((bf16[1536,24]{1,0:T(8,128)(2,1)}), bf16[96,24]{1,0:T(8,128)(2,1)}) %reduce-scatter.28.cloned.1.call-update) | async-done | bytes 4624
  2382.0 22.1 all-reduce.10.cloned.1.call-done
  (191 shorter events, 166.9 us)
Async XLA Ops:
  7.2 52.6 %copy-start.30 = (bf16[96,24]{0,1:T(8,128)(2,1)S(1)}, bf16[96,24]{0,1:T(8,128)(2,1)}, u32[]{:S(2)}) copy-start(bf16[96,24]{0,1:T(8,128)(2,1)} %param.24) | copy-start | bytes 13828
  7.2 90.3 %copy-start.33 = (s32[1,4]{1,0:T(1,128)S(1)}, s32[1,4]{1,0:T(1,128)}, u32[]{:S(2)}) copy-start(s32[1,4]{1,0:T(1,128)} %param.18) | copy-start | bytes 52
  7.2 90.3 %copy-start.32 = (s32[1,4]{1,0:T(1,128)S(1)}, s32[1,4]{1,0:T(1,128)}, u32[]{:S(2)}) copy-start(s32[1,4]{1,0:T(1,128)} %param.17) | copy-start | bytes 52
  7.3 90.4 %copy-start = (bf16[384,1536]{1,0:T(8,128)(2,1)S(1)}, bf16[384,1536]{1,0:T(8,128)(2,1)}, u32[]{:S(2)}) copy-start(bf16[384,1536]{1,0:T(8,128)(2,1)} %param.16) | copy-start | bytes 3538948
  7.3 92.6 %all-gather.12.cloned.1.call-start = ((), (), s32[]{:S(2)}) async-start(), calls=%async_computation.10 | async-start | bytes 5013504 | tf_op jit(solution)/shard_map/all_gather | solution.py:89
  8.0 168.4 %all-gather.14.cloned.1.call-start = ((), (), s32[]{:S(2)}) async-start(), calls=%async_computation.11 | async-start | bytes 5013504 | tf_op jit(solution)/shard_map/all_gather | solution.py:90
  8.7 248.8 %all-gather.10.cloned.1.call-start = ((), (), s32[]{:S(2)}) async-start(), calls=%async_computation.9 | async-start | bytes 5013504 | tf_op jit(solution)/shard_map/all_gather | solution.py:91
  9.5 329.1 %all-gather.16.cloned.1.call-start = ((), (), s32[]{:S(2)}) async-start(), calls=%async_computation.12 | async-start | bytes 5013504 | tf_op jit(solution)/shard_map/all_gather | solution.py:92
  10.1 409.6 %all-gather.18.cloned.1.call-start = ((), (), s32[]{:S(2)}) async-start(), calls=%async_computation.13 | async-start | bytes 5013504 | tf_op jit(solution)/shard_map/all_gather | solution.py:118
  10.6 561.7 %all-gather.22.cloned.1.call-start = ((), (), s32[]{:S(2)}) async-start(), calls=%async_computation.15 | async-start | bytes 13369344 | tf_op jit(solution)/shard_map/all_gather | solution.py:123
  11.2 713.6 %all-gather.20.cloned.1.call-start = ((), (), s32[]{:S(2)}) async-start(), calls=%async_computation.14 | async-start | bytes 13369344 | tf_op jit(solution)/shard_map/all_gather | solution.py:122
  12.0 865.2 %all-gather.24.cloned.1.call-start = ((), (), s32[]{:S(2)}) async-start(), calls=%async_computation.16 | async-start | bytes 13369344 | tf_op jit(solution)/shard_map/all_gather | solution.py:130
  12.7 1074.2 %reduce-scatter.20.cloned.1.call-start = ((), (), s32[]{:S(2)}) async-start(), calls=%async_computation.21 | async-start | bytes 5013504 | tf_op jit(solution)/shard_map/reduce_scatter | solution.py:233
  105.2 160.1 %copy-start.5 = (bf16[384,1536]{0,1:T(8,128)(2,1)}, bf16[384,1536]{0,1:T(8,128)(2,1)S(1)}, u32[]{:S(2)}) copy-start(bf16[384,1536]{0,1:T(8,128)(2,1)S(1)} %copy.67) | copy-start | bytes 3538948
  183.5 81.9 %copy-start.4 = (bf16[384,1536]{0,1:T(8,128)(2,1)}, bf16[384,1536]{0,1:T(8,128)(2,1)S(1)}, u32[]{:S(2)}) copy-start(bf16[384,1536]{0,1:T(8,128)(2,1)S(1)} %copy.68) | copy-start | bytes 3538948
  280.6 9.1 copy-start.22
  292.0 53.1 %copy-start.1 = (f32[384,1536]{1,0:T(8,128)}, f32[384,1536]{1,0:T(8,128)S(1)}, u32[]{:S(2)}) copy-start(f32[384,1536]{1,0:T(8,128)S(1)} %copy.71) | copy-start | bytes 7077892
  424.4 477.5 %copy-start.2 = (f32[384,1536]{1,0:T(8,128)}, f32[384,1536]{1,0:T(8,128)S(1)}, u32[]{:S(2)}) copy-start(f32[384,1536]{1,0:T(8,128)S(1)} %get-tuple-element.49) | copy-start | bytes 7077892
  892.2 9.8 copy-start.29
  892.2 9.8 copy-start.40
  902.0 9.3 copy-start.6
  918.1 279.3 %reduce-scatter.18.cloned.1.call-start = ((), (), s32[]{:S(2)}) async-start(), calls=%async_computation.20 | async-start | bytes 5013504 | tf_op jit(solution)/shard_map/reduce_scatter | solution.py:227
  918.2 7.9 copy-start.27
  930.6 410.2 %reduce-scatter.16.cloned.1.call-start = ((), (), s32[]{:S(2)}) async-start(), calls=%async_computation.19 | async-start | bytes 5013504 | tf_op jit(solution)/shard_map/reduce_scatter | solution.py:224
  948.4 535.3 %reduce-scatter.14.cloned.1.call-start = ((), (), s32[]{:S(2)}) async-start(), calls=%async_computation.18 | async-start | bytes 5013504 | tf_op jit(solution)/shard_map/reduce_scatter | solution.py:221
  984.5 642.2 %reduce-scatter.12.cloned.1.call-start = ((), (), s32[]{:S(2)}) async-start(), calls=%async_computation.17 | async-start | bytes 5013504 | tf_op jit(solution)/shard_map/reduce_scatter | solution.py:218
  997.1 836.9 %reduce-scatter.26.cloned.1.call-start = ((), (), s32[]{:S(2)}) async-start(), calls=%async_computation.24 | async-start | bytes 13369344 | tf_op jit(solution)/shard_map/reduce_scatter | solution.py:156
  1008.5 1033.2 %reduce-scatter.24.cloned.1.call-start = ((), (), s32[]{:S(2)}) async-start(), calls=%async_computation.23 | async-start | bytes 13369344 | tf_op jit(solution)/shard_map/reduce_scatter | solution.py:153
  1019.9 1229.5 %reduce-scatter.22.cloned.1.call-start = ((), (), s32[]{:S(2)}) async-start(), calls=%async_computation.22 | async-start | bytes 13369344 | tf_op jit(solution)/shard_map/reduce_scatter | solution.py:150
  1031.4 1345.7 %reduce-scatter.28.cloned.1.call-start = ((), (), s32[]{:S(2)}) async-start(), calls=%async_computation.25 | async-start | bytes 417792
  1037.0 1367.0 %all-reduce.10.cloned.1.call-start = ((), (), s32[]{:S(2)}) async-start(), calls=%async_computation.26 | async-start | bytes 7667712 | tf_op jit(solution)/shard_map/psum | solution.py:239
  2310.7 67.1 %copy-start.34 = (bf16[96]{0:T(256)(128)(2,1)S(1)}, bf16[96]{0:T(256)(128)(2,1)}, u32[]{:S(2)}) copy-start(bf16[96]{0:T(256)(128)(2,1)} %dynamic-slice.5) | copy-start | bytes 580
  (28 other events, 108.1 us)
Sparse Core Ops, SparseCore 0:
  10.9 83.8 all-gather.11
  97.6 78.7 all-gather.13
  179.2 78.3 all-gather.9
  260.2 78.3 all-gather.15
  341.3 78.3 all-gather.17
  422.3 150.0 all-gather.21
  575.2 149.5 all-gather.19
  727.6 149.5 all-gather.23
  918.3 136.5 reduce-scatter.19
  1059.9 137.4 reduce-scatter.17
  1202.6 138.0 reduce-scatter.15
  1345.8 137.8 reduce-scatter.13
  1488.8 137.8 reduce-scatter.11
  1632.2 201.6 reduce-scatter.25
  1839.5 202.1 reduce-scatter.23
  2047.2 202.1 reduce-scatter.21
  2254.5 122.4 reduce-scatter.27
  2379.7 24.2 all-reduce.9
where the time goes:
time: 2430 us; the launch traced here: 2420 us
  waiting for transfers between devices  1940 us (80%)
  matrix products  243 us (10%)
  blocking collectives  166 us (7%)
  other arithmetic  30.7 us (1%)
    reduce_scatter x1, waiting for transfers between devices, local(): lax.psum_scatter(grad_up_w.astype(jnp.bfloat16), 'shard', scatter_dimensi...  208 us
    reduce_scatter x1, waiting for transfers between devices, local(): lax.psum_scatter(grad_gate_w.astype(jnp.bfloat16), 'shard', scatter_dimen...  208 us
    reduce_scatter x1, waiting for transfers between devices, local(): lax.psum_scatter(grad_down.astype(jnp.bfloat16), 'shard', scatter_dimensi...  207 us
    all_gather x1, waiting for transfers between devices, local(): up_part = lax.all_gather(w_up, 'shard', axis=0, tiled=True)  146 us
    reduce_scatter x1, waiting for transfers between devices, local(): lax.psum_scatter(grad_value_w.astype(jnp.bfloat16), 'shard', scatter_dime...  143 us
    reduce_scatter x1, waiting for transfers between devices, local(): lax.psum_scatter(grad_query_w.astype(jnp.bfloat16), 'shard', scatter_dime...  143 us
    reduce_scatter x1, waiting for transfers between devices, local(): lax.psum_scatter(grad_key_w.astype(jnp.bfloat16), 'shard', scatter_dimens...  143 us
    all_gather x1, waiting for transfers between devices, local(): gate_part = lax.all_gather(w_gate, 'shard', axis=0, tiled=True)  142 us
  transfers between devices with their start and end apart: 18, of which 16 were waited for; matrix products, arithmetic and copies ran while one was open for 10% of the time, Pallas kernels for 0%

commit v1 on v0

--- a/solution.py
+++ b/solution.py
@@ -1,3 +1,4 @@
+import functools
 import jax
 import jax.numpy as jnp
 from jax import lax
@@ -9,6 +10,36 @@
 NC = 4
 EPS = 1e-06
 NEGATIVE = -1e30
+
+
+def take_core(buf, join_dim):
+    reply = jax.lax.axis_index("shard")
+    res = jax.lax.axis_size("shard")
+    u1, clean, prior = (res, reply, buf.shape[join_dim])
+    g_now = range(u1)
+    outcome_arr = map(lambda dev: (dev, (dev + 1) % u1), g_now)
+    by_place = list(outcome_arr)
+    current_value = range(u1)
+    shaped = map(lambda dev: (dev, (dev - 1) % u1), current_value)
+    t1 = jnp.zeros((*buf.shape[:join_dim], u1 * prior, *buf.shape[join_dim + 1 :]), buf.dtype)
+    t1 = lax.dynamic_update_slice_in_dim(t1, buf, clean * prior, axis=join_dim)
+    base_arr = passed = buf
+    mid_arr = u1 // 2
+    samples = list(shaped)
+    for dev_j in range(1, mid_arr + 1):
+        base_arr = jax.lax.ppermute(base_arr, "shard", by_place)
+        t1 = lax.dynamic_update_slice_in_dim(
+            t1, base_arr, (clean - dev_j) % u1 * prior, axis=join_dim
+        )
+        if dev_j < u1 - mid_arr:
+            passed = jax.lax.ppermute(passed, "shard", samples)
+            t1 = lax.dynamic_update_slice_in_dim(
+                t1, passed, (clean + dev_j) % u1 * prior, axis=join_dim
+            )
+    return t1
+
+
+classes_run = functools.partial(take_core, join_dim=0)
 
 
 def chain_mask(prompt_ids, offsets):
@@ -115,7 +146,7 @@
     ).reshape(row_count, model_width)
     gate_open = jax.nn.sigmoid(outgate_pre)
     gated_low = (attended * gate_open).astype(jnp.bfloat16)
-    branch_attn = matmul(gated_low, lax.all_gather(w_output, "shard", axis=0, tiled=True))
+    branch_attn = matmul(gated_low, classes_run(w_output))
     residual = inputs + branch_attn
     scaled2, inverse2 = normalize(residual)
     gain_part = lax.all_gather(ffn_gain, "shard", axis=0, tiled=True)

time: 2430 us -> 2470 us (1.016)
  starting transfers between devices: 0.97 us -> 41 us
    reduce_scatter x1, waiting for transfers between devices: 0.01 us -> 143 us  [local(): lax.psum_scatter(grad_output_w.astype(jnp.bfloat16), 'shard', scatter_dim...]
    reduce_scatter x1, waiting for transfers between devices: 143 us -> 8.03 us  [local(): lax.psum_scatter(grad_query_w.astype(jnp.bfloat16), 'shard', scatter_dime...]
    all_gather x1, waiting for transfers between devices: 74.1 us -> 0.01 us  [local(): value_part = lax.all_gather(w_value, 'shard', axis=0, tiled=True)]
    ppermute x0 -> x15, waiting for transfers between devices: none -> 65.7 us  [the longest x8 53.1 us: take_core(): base_arr = jax.lax.ppermute(base_arr, 'shard', by_place)]
    ppermute x0 -> x15, starting transfers between devices: none -> 40 us  [the longest x7 21.6 us: take_core(): passed = jax.lax.ppermute(passed, 'shard', samples)]
    reduce_scatter x1, waiting for transfers between devices: 110 us -> 143 us  [local(): lax.psum_scatter(grad_outgate_w.astype(jnp.bfloat16), 'shard', scatter_di...]
    all_gather x1, waiting for transfers between devices: 74.6 us -> 44.3 us  [local(): lax.all_gather(w_output, 'shard', axis=0, tiled=True)]
  transfers between devices with their start and end apart: 18 -> 33, of which waited for: 16 -> 25; matrix products, arithmetic and copies ran while one was open for 10% -> 10% of each run, Pallas kernels for 0% -> 0%
where the time goes in v1:
time: 2470 us
  waiting for transfers between devices  1940 us (79%)
  matrix products  245 us (10%)
  blocking collectives  166 us (7%)
  starting transfers between devices  41 us (2%)
  local copies, waits for them, and re-layouts  33.1 us (1%)
  other arithmetic  29.8 us (1%)
    reduce_scatter x1, waiting for transfers between devices, local(): lax.psum_scatter(grad_up_w.astype(jnp.bfloat16), 'shard', scatter_dimensi...  208 us
    reduce_scatter x1, waiting for transfers between devices, local(): lax.psum_scatter(grad_down.astype(jnp.bfloat16), 'shard', scatter_dimensi...  208 us
    reduce_scatter x1, waiting for transfers between devices, local(): lax.psum_scatter(grad_gate_w.astype(jnp.bfloat16), 'shard', scatter_dimen...  207 us
    reduce_scatter x1, waiting for transfers between devices, local(): lax.psum_scatter(grad_output_w.astype(jnp.bfloat16), 'shard', scatter_dim...  143 us
    reduce_scatter x1, waiting for transfers between devices, local(): lax.psum_scatter(grad_outgate_w.astype(jnp.bfloat16), 'shard', scatter_di...  143 us
    reduce_scatter x1, waiting for transfers between devices, local(): lax.psum_scatter(grad_key_w.astype(jnp.bfloat16), 'shard', scatter_dimens...  143 us
    reduce_scatter x1, waiting for transfers between devices, local(): lax.psum_scatter(grad_value_w.astype(jnp.bfloat16), 'shard', scatter_dime...  143 us
    all_gather x1, waiting for transfers between devices, local(): lax.all_gather(w_down, 'shard', axis=0, tiled=True)  142 us
  transfers between devices with their start and end apart: 33, of which 25 were waited for; matrix products, arithmetic and copies ran while one was open for 10% of the time, Pallas kernels for 0%

profile of v1, /device:TPU:0, one launch (start us, length us, event | category | flops | bytes accessed | tf_op | source)
XLA Modules:
  0.0 2469.0 jit_solution(5328671414272763971)
XLA Ops:
  21.0 44.5 %all-reduce.5 = (bf16[1536]{0:T(1024)(128)(2,1)S(1)}, bf16[1536]{0:T(1024)(128)(2,1)S(1)}) all-reduce(bf16[1536]{0:T(1024)(128)(2,1)S(1)} %dynamic-update-slice, bf16[1536]{0:T(1024)(128)(2,1)S(1)} %dynamic-update-slice.1), channel_id=1, replica_groups=mesh['rep'=2,'shard'=16] {'shard'}, use_global_device_ids=true, to_apply=%add | all-reduce | flops 3072 | bytes 12288
  66.0 37.6 %all-gather = bf16[16,96,24]{1,2,0:T(8,128)(2,1)S(1)} all-gather(bf16[1,96,24]{1,2,0:T(8,128)(2,1)S(1)} %bitcast.93), channel_id=1, replica_groups=mesh['rep'=2,'shard'=16] {'shard'}, dimensions={0}, use_global_device_ids=true | all-gather | bytes 78336 | tf_op jit(solution)/shard_map/all_gather | solution.py:124
  163.4 10.9 collective-permute-done.8
  181.3 11.6 collective-permute-done.10
  229.6 70.0 %all-gather.14.cloned.1.call-done = bf16[1536,1536]{1,0:T(8,128)(2,1)} async-done(((bf16[96,1536]{1,0:T(8,128)(2,1)}), bf16[1536,1536]{1,0:T(8,128)(2,1)}) %all-gather.14.cloned.1.call-update) | async-done | bytes 4718608 | tf_op jit(solution)/shard_map/all_gather | solution.py:121
  322.9 9.1 fusion.10
  334.2 46.4 %all-gather.16.cloned.1.call-done = bf16[1536,1536]{1,0:T(8,128)(2,1)} async-done(((bf16[96,1536]{1,0:T(8,128)(2,1)}), bf16[1536,1536]{1,0:T(8,128)(2,1)}) %all-gather.16.cloned.1.call-update) | async-done | bytes 4718608 | tf_op jit(solution)/shard_map/all_gather | solution.py:123
  393.4 139.9 %all-gather.18.cloned.1.call-done = bf16[1536,4096]{1,0:T(8,128)(2,1)} async-done(((bf16[96,4096]{1,0:T(8,128)(2,1)}), bf16[1536,4096]{1,0:T(8,128)(2,1)}) %all-gather.18.cloned.1.call-update) | async-done | bytes 12582928 | tf_op jit(solution)/shard_map/all_gather | solution.py:153
  533.3 10.0 fusion.87
  543.3 142.3 %all-gather.20.cloned.1.call-done = bf16[1536,4096]{1,0:T(8,128)(2,1)} async-done(((bf16[96,4096]{1,0:T(8,128)(2,1)}), bf16[1536,4096]{1,0:T(8,128)(2,1)}) %all-gather.20.cloned.1.call-update) | async-done | bytes 12582928 | tf_op jit(solution)/shard_map/all_gather | solution.py:154
  685.6 10.0 fusion.88
  695.5 142.4 %all-gather.22.cloned.1.call-done = bf16[4096,1536]{1,0:T(8,128)(2,1)} async-done(((bf16[256,1536]{1,0:T(8,128)(2,1)}), bf16[4096,1536]{1,0:T(8,128)(2,1)}) %all-gather.22.cloned.1.call-update) | async-done | bytes 12582928 | tf_op jit(solution)/shard_map/all_gather | solution.py:161
  838.0 15.2 multiply_convert_fusion.1
  853.2 9.4 fusion.89
  862.7 9.3 multiply_reduce_fusion.1
  874.3 44.3 %all-gather.24.cloned.1.call-done = bf16[1536,1536]{1,0:T(8,128)(2,1)} async-done(((bf16[96,1536]{1,0:T(8,128)(2,1)}), bf16[1536,1536]{1,0:T(8,128)(2,1)}) %all-gather.24.cloned.1.call-update) | async-done | bytes 4718608 | tf_op jit(solution)/shard_map/all_gather | solution.py:195
  928.3 22.3 fusion.83
  1002.2 11.6 convolution_convert_fusion.2
  1013.9 11.3 convolution_convert_fusion.1
  1025.3 11.3 convolution_convert_fusion
  1053.4 40.0 %psum.90 = f32[24]{0:T(128)} all-reduce(f32[24]{0:T(128)S(1)} %get-tuple-element.53), channel_id=1, replica_groups=mesh['rep'=2,'shard'=16] {'rep','shard'}, use_global_device_ids=true, to_apply=%region_25.26 | all-reduce | flops 24 | bytes 192 | tf_op jit(solution)/shard_map/psum | solution.py:219
  1101.4 142.8 %reduce-scatter.14.cloned.1.call-done = bf16[96,1536]{1,0:T(8,128)(2,1)} async-done(((bf16[1536,1536]{1,0:T(8,128)(2,1)}), bf16[96,1536]{1,0:T(8,128)(2,1)}) %reduce-scatter.14.cloned.1.call-update) | async-done | bytes 294928 | tf_op jit(solution)/shard_map/reduce_scatter | solution.py:252
  1244.3 142.6 %reduce-scatter.16.cloned.1.call-done = bf16[96,1536]{1,0:T(8,128)(2,1)} async-done(((bf16[1536,1536]{1,0:T(8,128)(2,1)}), bf16[96,1536]{1,0:T(8,128)(2,1)}) %reduce-scatter.16.cloned.1.call-update) | async-done | bytes 294928 | tf_op jit(solution)/shard_map/reduce_scatter | solution.py:255
  1386.9 142.9 %reduce-scatter.18.cloned.1.call-done = bf16[96,1536]{1,0:T(8,128)(2,1)} async-done(((bf16[1536,1536]{1,0:T(8,128)(2,1)}), bf16[96,1536]{1,0:T(8,128)(2,1)}) %reduce-scatter.18.cloned.1.call-update) | async-done | bytes 294928 | tf_op jit(solution)/shard_map/reduce_scatter | solution.py:258
  1529.8 143.4 %reduce-scatter.20.cloned.1.call-done = bf16[96,1536]{1,0:T(8,128)(2,1)} async-done(((bf16[1536,1536]{1,0:T(8,128)(2,1)}), bf16[96,1536]{1,0:T(8,128)(2,1)}) %reduce-scatter.20.cloned.1.call-update) | async-done | bytes 294928 | tf_op jit(solution)/shard_map/reduce_scatter | solution.py:264
  1673.2 207.2 %reduce-scatter.22.cloned.1.call-done = bf16[96,4096]{1,0:T(8,128)(2,1)} async-done(((bf16[1536,4096]{1,0:T(8,128)(2,1)}), bf16[96,4096]{1,0:T(8,128)(2,1)}) %reduce-scatter.22.cloned.1.call-update) | async-done | bytes 786448 | tf_op jit(solution)/shard_map/reduce_scatter | solution.py:181
  1880.3 207.9 %reduce-scatter.24.cloned.1.call-done = bf16[96,4096]{1,0:T(8,128)(2,1)} async-done(((bf16[1536,4096]{1,0:T(8,128)(2,1)}), bf16[96,4096]{1,0:T(8,128)(2,1)}) %reduce-scatter.24.cloned.1.call-update) | async-done | bytes 786448 | tf_op jit(solution)/shard_map/reduce_scatter | solution.py:184
  2088.2 207.8 %reduce-scatter.26.cloned.1.call-done = bf16[256,1536]{1,0:T(8,128)(2,1)} async-done(((bf16[4096,1536]{1,0:T(8,128)(2,1)}), bf16[256,1536]{1,0:T(8,128)(2,1)}) %reduce-scatter.26.cloned.1.call-update) | async-done | bytes 786448 | tf_op jit(solution)/shard_map/reduce_scatter | solution.py:187
  2309.0 41.8 %all-reduce.4 = (bf16[1536]{0:T(1024)(128)(2,1)}, bf16[1536]{0:T(1024)(128)(2,1)}) all-reduce(bf16[1536]{0:T(1024)(128)(2,1)S(1)} %get-tuple-element.18, bf16[1536]{0:T(1024)(128)(2,1)} %get-tuple-element.16), channel_id=2, replica_groups=mesh['rep'=2,'shard'=16] {'shard'}, use_global_device_ids=true, to_apply=%region_12.13.clone | all-reduce | flops 3072 | bytes 12288
  2357.3 9.3 fusion.19
  2366.6 56.9 %reduce-scatter.28.cloned.1.call-done = bf16[96,24]{1,0:T(8,128)(2,1)} async-done(((bf16[1536,24]{1,0:T(8,128)(2,1)}), bf16[96,24]{1,0:T(8,128)(2,1)}) %reduce-scatter.28.cloned.1.call-update) | async-done | bytes 4624
  2428.5 22.1 all-reduce.10.cloned.1.call-done
  (236 shorter events, 278.5 us)
Async XLA Ops:
  7.2 211.4 %all-gather.10.cloned.1.call-start = ((), (), s32[]{:S(2)}) async-start(), calls=%async_computation.9 | async-start | bytes 5013504 | tf_op jit(solution)/shard_map/all_gather | solution.py:122
  8.0 216.4 %all-gather.12.cloned.1.call-start = ((), (), s32[]{:S(2)}) async-start(), calls=%async_computation.10 | async-start | bytes 5013504 | tf_op jit(solution)/shard_map/all_gather | solution.py:120
  8.7 290.8 %all-gather.14.cloned.1.call-start = ((), (), s32[]{:S(2)}) async-start(), calls=%async_computation.11 | async-start | bytes 5013504 | tf_op jit(solution)/shard_map/all_gather | solution.py:121
  9.5 371.1 %all-gather.16.cloned.1.call-start = ((), (), s32[]{:S(2)}) async-start(), calls=%async_computation.12 | async-start | bytes 5013504 | tf_op jit(solution)/shard_map/all_gather | solution.py:123
  10.1 523.2 %all-gather.18.cloned.1.call-start = ((), (), s32[]{:S(2)}) async-start(), calls=%async_computation.13 | async-start | bytes 13369344 | tf_op jit(solution)/shard_map/all_gather | solution.py:153
  10.7 674.9 %all-gather.20.cloned.1.call-start = ((), (), s32[]{:S(2)}) async-start(), calls=%async_computation.14 | async-start | bytes 13369344 | tf_op jit(solution)/shard_map/all_gather | solution.py:154
  11.2 826.7 %all-gather.22.cloned.1.call-start = ((), (), s32[]{:S(2)}) async-start(), calls=%async_computation.15 | async-start | bytes 13369344 | tf_op jit(solution)/shard_map/all_gather | solution.py:161
  12.0 906.7 %all-gather.24.cloned.1.call-start = ((), (), s32[]{:S(2)}) async-start(), calls=%async_computation.16 | async-start | bytes 5013504 | tf_op jit(solution)/shard_map/all_gather | solution.py:195
  12.0 96.9 %collective-permute-start = (bf16[96,1536]{1,0:T(8,128)(2,1)S(1)}, bf16[96,1536]{1,0:T(8,128)(2,1)S(1)}, u32[]{:S(2)}, u32[]{:S(2)}) collective-permute-start(bf16[96,1536]{1,0:T(8,128)(2,1)S(1)} %copy-done.13), channel_id=1, source_target_pairs={{0,1},{1,2},{2,3},{3,4},{4,5},{5,6},{6,7},{7,8},{8,9},{9,10},{10,1... | collective-permute-start | bytes 884744 | tf_op jit(solution)/shard_map/ppermute | solution.py:30
  15.1 95.8 %collective-permute-start.1 = (bf16[96,1536]{1,0:T(8,128)(2,1)S(1)}, bf16[96,1536]{1,0:T(8,128)(2,1)S(1)}, u32[]{:S(2)}, u32[]{:S(2)}) collective-permute-start(bf16[96,1536]{1,0:T(8,128)(2,1)S(1)} %copy-done.13), channel_id=1, source_target_pairs={{0,15},{1,0},{2,1},{3,2},{4,3},{5,4},{6,5},{7,6},{8,7},{9,8},{10,9... | collective-permute-start | bytes 884744 | tf_op jit(solution)/shard_map/ppermute | solution.py:35
  19.1 1082.3 %reduce-scatter.12.cloned.1.call-start = ((), (), s32[]{:S(2)}) async-start(), calls=%async_computation.17 | async-start | bytes 5013504 | tf_op jit(solution)/shard_map/reduce_scatter | solution.py:249
  108.9 14.9 collective-permute-start.2
  110.9 15.5 collective-permute-start.3
  123.9 15.5 collective-permute-start.4
  126.3 15.5 collective-permute-start.5
  139.4 16.9 collective-permute-start.6
  141.8 16.9 collective-permute-start.7
  156.2 18.0 collective-permute-start.8
  158.7 18.0 collective-permute-start.9
  174.2 18.7 collective-permute-start.10
  176.7 25.7 %collective-permute-start.11 = (bf16[96,1536]{1,0:T(8,128)(2,1)S(1)}, bf16[96,1536]{1,0:T(8,128)(2,1)S(1)}, u32[]{:S(2)}, u32[]{:S(2)}) collective-permute-start(bf16[96,1536]{1,0:T(8,128)(2,1)S(1)} %collective-permute-done.9), channel_id=1, source_target_pairs={{0,15},{1,0},{2,1},{3,2},{4,3},{5,4},{6,5},{7,6},{8,7},{9,8},{10,9... | collective-permute-start | bytes 884744 | tf_op jit(solution)/shard_map/ppermute | solution.py:35
  193.0 12.4 collective-permute-start.12
  205.4 12.5 collective-permute-start.14
  963.2 281.1 %reduce-scatter.14.cloned.1.call-start = ((), (), s32[]{:S(2)}) async-start(), calls=%async_computation.18 | async-start | bytes 5013504 | tf_op jit(solution)/shard_map/reduce_scatter | solution.py:252
  976.9 410.0 %reduce-scatter.16.cloned.1.call-start = ((), (), s32[]{:S(2)}) async-start(), calls=%async_computation.19 | async-start | bytes 5013504 | tf_op jit(solution)/shard_map/reduce_scatter | solution.py:255
  990.6 539.1 %reduce-scatter.18.cloned.1.call-start = ((), (), s32[]{:S(2)}) async-start(), calls=%async_computation.20 | async-start | bytes 5013504 | tf_op jit(solution)/shard_map/reduce_scatter | solution.py:258
  996.5 676.7 %reduce-scatter.20.cloned.1.call-start = ((), (), s32[]{:S(2)}) async-start(), calls=%async_computation.21 | async-start | bytes 5013504 | tf_op jit(solution)/shard_map/reduce_scatter | solution.py:264
  1002.2 878.2 %reduce-scatter.22.cloned.1.call-start = ((), (), s32[]{:S(2)}) async-start(), calls=%async_computation.22 | async-start | bytes 13369344 | tf_op jit(solution)/shard_map/reduce_scatter | solution.py:181
  1013.8 1074.4 %reduce-scatter.24.cloned.1.call-start = ((), (), s32[]{:S(2)}) async-start(), calls=%async_computation.23 | async-start | bytes 13369344 | tf_op jit(solution)/shard_map/reduce_scatter | solution.py:184
  1025.2 1270.8 %reduce-scatter.26.cloned.1.call-start = ((), (), s32[]{:S(2)}) async-start(), calls=%async_computation.24 | async-start | bytes 13369344 | tf_op jit(solution)/shard_map/reduce_scatter | solution.py:187
  1036.6 1386.9 %reduce-scatter.28.cloned.1.call-start = ((), (), s32[]{:S(2)}) async-start(), calls=%async_computation.25 | async-start | bytes 417792
  1042.3 1408.3 %all-reduce.10.cloned.1.call-start = ((), (), s32[]{:S(2)}) async-start(), calls=%async_computation.26 | async-start | bytes 7667712 | tf_op jit(solution)/shard_map/psum | solution.py:270
  (42 other events, 1327.5 us)
Sparse Core Ops, SparseCore 0:
  10.8 89.8 all-gather.9
  103.5 111.4 all-gather.11
  217.9 81.6 all-gather.13
  302.2 78.3 all-gather.15
  383.2 150.0 all-gather.17
  535.9 149.5 all-gather.19
  688.3 149.5 all-gather.21
  840.8 77.8 all-gather.23
  963.3 138.0 reduce-scatter.11
  1106.5 137.7 reduce-scatter.13
  1249.5 137.4 reduce-scatter.15
  1391.9 137.8 reduce-scatter.17
  1535.0 138.1 reduce-scatter.19
  1678.7 201.6 reduce-scatter.21
  1885.8 202.3 reduce-scatter.23
  2093.7 202.2 reduce-scatter.25
  2301.1 122.4 reduce-scatter.27
  2426.3 24.2 all-reduce.9
